TPU v7x, 128 devices: a whole 4x4x4 slice. The times are simulated.
128 devices in a mesh: row: 8 (over z, core), col: 16 (over y, x).
Axes of the slice: x: 4, y: 4, z: 4, core: 2. Of those that a mesh axis runs over, the one named last changes fastest.
Arguments:
- amp_tiles: float32 [16, 32, 256, 256], P('row', 'col'), may hold values from -6 to 6
- int_tiles: float32 [32, 32, 256, 256], P('col', 'row'), may hold values from -0.125 to 0.125
- resid_init: float32 [16, 32, 256, 256], P('row', 'col'), may hold values from -6 to 6
- triples: int32 [8, 16, 3, 32], P('row', 'col'), may hold values from 0 to 1023, as said below
Outputs:
- resid_out: float32 [16, 32, 256, 256], P('row', 'col')
Inputs may be any that keep to these rules, and one draw needn't show every extreme that they name: Each triple names tiles (i, j), (j, k), (i, k) with one i, j, k. The amplitude tile of every triple on device (r, c) is one that device holds. For every device and every column index q, exactly 2 distinct residual tiles held at (r, q) are named by that device's triples, each by exactly one of that device's triples. No triple is listed twice; the order of triples on a device is arbitrary.
All inputs are finite; a program needn't handle non-finite values.
Results may differ from a plain program's by a relative error of at most 0.0001.
Values sent between devices are 32-bit elements; how exact they have to be, the bound alone decides.
No kernel may reach another device: no remote copies, remote signals or barrier semaphores. Data moves between devices by JAX's collectives and lax.ppermute only.
A program may use at most 128 MiB of HBM per device.

v0:
```python
import jax
import jax.numpy as jnp
from jax import lax
from jax.sharding import PartitionSpec as P


def on_device(amp_tiles, int_tiles, resid_init, triples):
    occ_blocks = amp_tiles.shape[0]
    vir_blocks = amp_tiles.shape[1]
    width = amp_tiles.shape[2]
    own_k = resid_init.shape[1]
    col_count = lax.axis_size("col")
    all_k = own_k * col_count
    all_j = vir_blocks * col_count
    row_place = lax.axis_index("row")
    col_place = lax.axis_index("col")
    listing = triples[0, 0]
    amp_ids = listing[0]
    int_ids = listing[1]
    res_ids = listing[2]
    amp_occ = amp_ids // all_j - row_place * occ_blocks
    amp_vir = amp_ids % all_j - col_place * vir_blocks
    int_vir = int_ids // all_k - col_place * vir_blocks
    int_col = int_ids % all_k
    res_occ = res_ids // all_k - row_place * occ_blocks
    res_col = res_ids % all_k
    amp_index = amp_occ * vir_blocks + amp_vir
    int_index = int_vir * all_k + int_col
    gathered = lax.all_gather(int_tiles, "row", axis=1, tiled=True)
    amp_flat = amp_tiles.reshape(-1, width, width)
    int_flat = gathered.reshape(-1, width, width)
    target = res_occ * all_k + res_col
    slots_total = occ_blocks * all_k
    block = 8

    def add_block(partial_value, pieces):
        amp_pick, int_pick, target_pick = pieces
        products = jnp.einsum(
            "bxy,byz->bxz",
            amp_flat[amp_pick],
            int_flat[int_pick],
            precision=lax.Precision.HIGHEST,
            preferred_element_type=jnp.float32,
        )
        return (partial_value.at[target_pick].add(products), None)

    start = jnp.zeros((slots_total, width, width), jnp.float32)
    pieces = (amp_index.reshape(-1, block), int_index.reshape(-1, block), target.reshape(-1, block))
    partial_value, _ = lax.scan(add_block, start, pieces)
    summed = lax.psum_scatter(
        partial_value.reshape(occ_blocks, all_k, width, width),
        "col",
        scatter_dimension=1,
        tiled=True,
    )
    return resid_init + summed


def solution(mesh):
    return jax.shard_map(
        on_device,
        mesh=mesh,
        in_specs=(
            P("row", "col", None, None),
            P("col", "row", None, None),
            P("row", "col", None, None),
            P("row", "col", None, None),
        ),
        out_specs=P("row", "col", None, None),
        check_vma=False,
    )
```

profile of v0, /device:TPU:1, one launch (start us, length us, event | category | flops | bytes accessed | tf_op | source)
XLA Modules:
  0.0 409.5 jit_solution(13803242583573978467)
XLA Ops:
  6.5 0.0 all-gather.2.cloned.1.call-start
  6.5 0.7 all-gather.2.cloned.1.call-update
  7.3 0.0 all-reduce.3.cloned.1.call-start
  7.3 0.0 copy-done.2
  7.3 0.1 squeeze.20
  7.4 0.1 squeeze.21
  7.5 0.1 squeeze.22
  7.6 90.2 %all-gather.2.cloned.1.call-done = f32[2,32,256,256]{3,2,1,0:T(8,128)} async-done(((f32[2,4,256,256]{3,2,1,0:T(8,128)}), f32[2,32,256,256]{3,2,1,0:T(8,128)}) %all-gather.2.cloned.1.call-update) | async-done | bytes 16777232 | tf_op jit(solution)/shard_map/all_gather | solution.py:29
  97.9 7.8 %broadcast_in_dim.2 = f32[64,256,256]{2,1,0:T(8,128)} broadcast(f32[]{:T(128)} %constant.72.clone.1), dimensions={} | broadcast | bytes 16777220 | tf_op jit(solution)/shard_map/broadcast_in_dim | solution.py:47
  105.6 0.0 copy-done
  105.6 74.2 %while.10 = (s32[]{:T(128)}, f32[64,256,256]{2,1,0:T(8,128)}, s32[4,8]{1,0:T(4,128)S(1)}, s32[4,8]{1,0:T(4,128)S(1)}, f32[4,256,256]{2,1,0:T(8,128)S(1)}, /*inde...) while((s32[]{:T(128)}, f32[64,256,256]{2,1,0:T(8,128)}, s32[4,8]{1,0:T(4,128)S(1)}, ...), condition=%wide.region_2.3_spmd, body=%wide.region_0.2_spmd.sunk | while | flops 1611139200 | bytes 20980156 | solution.py:49
  105.7 2.0 gather_fusion
  107.7 7.8 %gather_fusion.1 = f32[8,256,256]{2,1,0:T(8,128)} fusion(f32[64,256,256]{2,1,0:T(8,128)} %get-tuple-element.133, s32[1024]{0:T(1024)S(1)} %pad_clamp_fusion.5), kind=kCustom, calls=%fused_computation.1.clone.1 | custom fusion | bytes 4194336 | tf_op jit(solution)/shard_map/while/body/eval_jaxpr/gather | solution.py:41
  115.5 4.3 %fusion.34 = f32[8,256,256]{2,1,0:T(8,128)S(1)} fusion(f32[8,256,256]{2,1,0:T(8,128)} %gather_fusion, f32[8,256,256]{2,1,0:T(8,128)} %gather_fusion.1), kind=kOutput, calls=%fused_computation.55.clone.1 | convolution fusion | flops 1610612736 | bytes 6291456 | tf_op jit(solution)/shard_map/while/body/eval_jaxpr/bxy,byz->bxz/dot_general | solution.py:38
  119.8 4.4 %scatter_fusion = f32[64,256,256]{2,1,0:T(8,128)} fusion(f32[64,256,256]{2,1,0:T(8,128)} %get-tuple-element.120, s32[8]{0:T(128)S(1)} %get-tuple-element.109, f32[8,256,256]{2,1,0:T(8,128)S(1)} %fusion.34), kind=kCustom, calls=%fused_computation.2.clone.1 | custom fusion | flops 524288 | bytes 6291488 | tf_op jit(solution)/shard_map/while/body/eval_jaxpr/scatter-add | solution.py:45
  124.2 2.0 gather_fusion
  126.2 7.8 %gather_fusion.1 = f32[8,256,256]{2,1,0:T(8,128)} fusion(f32[64,256,256]{2,1,0:T(8,128)} %get-tuple-element.133, s32[1024]{0:T(1024)S(1)} %pad_clamp_fusion.5), kind=kCustom, calls=%fused_computation.1.clone.1 | custom fusion | bytes 4194336 | tf_op jit(solution)/shard_map/while/body/eval_jaxpr/gather | solution.py:41
  134.0 4.3 %fusion.34 = f32[8,256,256]{2,1,0:T(8,128)S(1)} fusion(f32[8,256,256]{2,1,0:T(8,128)} %gather_fusion, f32[8,256,256]{2,1,0:T(8,128)} %gather_fusion.1), kind=kOutput, calls=%fused_computation.55.clone.1 | convolution fusion | flops 1610612736 | bytes 6291456 | tf_op jit(solution)/shard_map/while/body/eval_jaxpr/bxy,byz->bxz/dot_general | solution.py:38
  138.3 4.4 %scatter_fusion = f32[64,256,256]{2,1,0:T(8,128)} fusion(f32[64,256,256]{2,1,0:T(8,128)} %get-tuple-element.120, s32[8]{0:T(128)S(1)} %get-tuple-element.109, f32[8,256,256]{2,1,0:T(8,128)S(1)} %fusion.34), kind=kCustom, calls=%fused_computation.2.clone.1 | custom fusion | flops 524288 | bytes 6291488 | tf_op jit(solution)/shard_map/while/body/eval_jaxpr/scatter-add | solution.py:45
  142.8 2.0 gather_fusion
  144.8 7.8 %gather_fusion.1 = f32[8,256,256]{2,1,0:T(8,128)} fusion(f32[64,256,256]{2,1,0:T(8,128)} %get-tuple-element.133, s32[1024]{0:T(1024)S(1)} %pad_clamp_fusion.5), kind=kCustom, calls=%fused_computation.1.clone.1 | custom fusion | bytes 4194336 | tf_op jit(solution)/shard_map/while/body/eval_jaxpr/gather | solution.py:41
  152.6 4.3 %fusion.34 = f32[8,256,256]{2,1,0:T(8,128)S(1)} fusion(f32[8,256,256]{2,1,0:T(8,128)} %gather_fusion, f32[8,256,256]{2,1,0:T(8,128)} %gather_fusion.1), kind=kOutput, calls=%fused_computation.55.clone.1 | convolution fusion | flops 1610612736 | bytes 6291456 | tf_op jit(solution)/shard_map/while/body/eval_jaxpr/bxy,byz->bxz/dot_general | solution.py:38
  156.9 4.4 %scatter_fusion = f32[64,256,256]{2,1,0:T(8,128)} fusion(f32[64,256,256]{2,1,0:T(8,128)} %get-tuple-element.120, s32[8]{0:T(128)S(1)} %get-tuple-element.109, f32[8,256,256]{2,1,0:T(8,128)S(1)} %fusion.34), kind=kCustom, calls=%fused_computation.2.clone.1 | custom fusion | flops 524288 | bytes 6291488 | tf_op jit(solution)/shard_map/while/body/eval_jaxpr/scatter-add | solution.py:45
  161.3 2.0 gather_fusion
  163.3 7.8 %gather_fusion.1 = f32[8,256,256]{2,1,0:T(8,128)} fusion(f32[64,256,256]{2,1,0:T(8,128)} %get-tuple-element.133, s32[1024]{0:T(1024)S(1)} %pad_clamp_fusion.5), kind=kCustom, calls=%fused_computation.1.clone.1 | custom fusion | bytes 4194336 | tf_op jit(solution)/shard_map/while/body/eval_jaxpr/gather | solution.py:41
  171.2 4.3 %fusion.34 = f32[8,256,256]{2,1,0:T(8,128)S(1)} fusion(f32[8,256,256]{2,1,0:T(8,128)} %gather_fusion, f32[8,256,256]{2,1,0:T(8,128)} %gather_fusion.1), kind=kOutput, calls=%fused_computation.55.clone.1 | convolution fusion | flops 1610612736 | bytes 6291456 | tf_op jit(solution)/shard_map/while/body/eval_jaxpr/bxy,byz->bxz/dot_general | solution.py:38
  175.5 4.4 %scatter_fusion = f32[64,256,256]{2,1,0:T(8,128)} fusion(f32[64,256,256]{2,1,0:T(8,128)} %get-tuple-element.120, s32[8]{0:T(128)S(1)} %get-tuple-element.109, f32[8,256,256]{2,1,0:T(8,128)S(1)} %fusion.34), kind=kCustom, calls=%fused_computation.2.clone.1 | custom fusion | flops 524288 | bytes 6291488 | tf_op jit(solution)/shard_map/while/body/eval_jaxpr/scatter-add | solution.py:45
  179.8 0.0 all-reduce.3.cloned.1.call-update
  179.9 0.6 copy-done.3
  180.5 0.6 dynamic-slice
  181.7 218.7 %all-reduce.3.cloned.1.call-done = f32[2,32,256,256]{3,2,1,0:T(8,128)} async-done(((f32[2,32,256,256]{3,2,1,0:T(8,128)}), f32[2,32,256,256]{3,2,1,0:T(8,128)}) %all-reduce.3.cloned.1.call-update) | async-done | bytes 16777232
  400.4 2.3 dynamic-slice_add_fusion
  (24 shorter events, 0.2 us)
Async XLA Ops:
  6.5 0.8 copy-start.2
  6.5 91.3 %all-gather.2.cloned.1.call-start = ((), (), s32[]{:S(2)}) async-start(), calls=%async_computation | async-start | bytes 18874368 | tf_op jit(solution)/shard_map/all_gather | solution.py:29
  7.3 393.1 %all-reduce.3.cloned.1.call-start = ((), (), s32[]{:S(2)}) async-start(), calls=%async_computation.1 | async-start | bytes 33554432
  97.9 7.8 %copy-start = (f32[2,2,256,256]{3,2,1,0:T(8,128)S(1)}, f32[2,2,256,256]{3,2,1,0:T(8,128)}, u32[]{:S(2)}) copy-start(f32[2,2,256,256]{3,2,1,0:T(8,128)} %param.6) | copy-start | bytes 3145732
  179.8 0.7 copy-start.3
  179.8 220.5 %copy-start.1 = (f32[2,2,256,256]{3,2,1,0:T(8,128)S(1)}, f32[2,2,256,256]{3,2,1,0:T(8,128)}, u32[]{:S(2)}) copy-start(f32[2,2,256,256]{3,2,1,0:T(8,128)} %param.8) | copy-start | bytes 3145732
Sparse Core Ops, SparseCore 0:
  9.1 88.7 all-gather.1
  180.0 220.3 all-reduce.2
where the time goes:
time: 410 us
  waiting for transfers between devices  310 us (76%)
  local copies, waits for them, and re-layouts  48.5 us (12%)
  other arithmetic  20 us (5%)
  matrix products  17.2 us (4%)
  between operations  14.1 us (3%)
    unnamed x3, waiting for transfers between devices  219 us
    all_gather x1, waiting for transfers between devices, on_device(): gathered = lax.all_gather(int_tiles, 'row', axis=1, tiled=True)  90.2 us
    gather x4, local copies, waits for them, and re-layouts, add_block(): int_flat[int_pick]  31.3 us
    scatter-add x4, other arithmetic, add_block(): return (partial_value.at[target_pick].add(products), None)  17.5 us
    dot_general x4, matrix products, add_block(): jnp.einsum('bxy,byz->bxz', amp_flat[amp_pick], int_flat[int_pick], precis...  17.2 us
  transfers between devices with their start and end apart: 2, of which 2 were waited for; matrix products, arithmetic and copies ran while one was open for 0% of the time, Pallas kernels for 0%

commit v1 on v0

--- a/solution.py
+++ b/solution.py
@@ -2,6 +2,19 @@
 import jax.numpy as jnp
 from jax import lax
 from jax.sharding import PartitionSpec as P
+
+
+def ring_gather(array, axis, dim):
+    ways = lax.axis_size(axis)
+    up = [(d, (d + 1) % ways) for d in range(ways)]
+    down = [(d, (d - 1) % ways) for d in range(ways)]
+    earlier, later = ([array], [array])
+    for _ in range(ways // 2):
+        earlier.append(lax.ppermute(earlier[-1], axis, up))
+    for _ in range((ways - 1) // 2):
+        later.append(lax.ppermute(later[-1], axis, down))
+    line = jnp.concatenate([*earlier[::-1], *later[1:]], axis=dim)
+    return jnp.roll(line, (lax.axis_index(axis) - ways // 2) * array.shape[dim], axis=dim)
 
 
 def on_device(amp_tiles, int_tiles, resid_init, triples):
@@ -26,7 +39,7 @@
     res_col = res_ids % all_k
     amp_index = amp_occ * vir_blocks + amp_vir
     int_index = int_vir * all_k + int_col
-    gathered = lax.all_gather(int_tiles, "row", axis=1, tiled=True)
+    gathered = ring_gather(int_tiles, "row", 1)
     amp_flat = amp_tiles.reshape(-1, width, width)
     int_flat = gathered.reshape(-1, width, width)
     target = res_occ * all_k + res_col

time: 410 us -> 454 us (1.11)
  local copies, waits for them, and re-layouts: 48.5 us -> 77.8 us
  starting transfers between devices: 0.04 us -> 13.8 us
    all_gather x1 -> x0, waiting for transfers between devices: 90.2 us -> none  [on_device(): gathered = lax.all_gather(int_tiles, 'row', axis=1, tiled=True)]
    ppermute x0 -> x7, waiting for transfers between devices: none -> 86.8 us  [the longest x4 84.2 us: ring_gather(): earlier.append(lax.ppermute(earlier[-1], axis, up))]
    unnamed x9 -> x36, local copies, waits for them, and re-layouts: 1.22 us -> 21.5 us
    ppermute x0 -> x7, starting transfers between devices: none -> 13.8 us  [the longest x4 10.5 us: ring_gather(): earlier.append(lax.ppermute(earlier[-1], axis, up))]
    dynamic_slice x0 -> x1, local copies, waits for them, and re-layouts: none -> 6.35 us  [ring_gather(): jnp.roll(line, (lax.axis_index(axis) - ways // 2) * array.shape[dim], axi...]
    unnamed x3 -> x2, waiting for transfers between devices: 219 us -> 223 us
  transfers between devices with their start and end apart: 2 -> 8, of which waited for: 2 -> 7; matrix products, arithmetic and copies ran while one was open for 0% -> 2% of each run, Pallas kernels for 0% -> 0%
where the time goes in v1:
time: 454 us; the launch traced here: 453 us
  waiting for transfers between devices  310 us (68%)
  local copies, waits for them, and re-layouts  77.8 us (17%)
  other arithmetic  20 us (4%)
  matrix products  17.2 us (4%)
  between operations  14.3 us (3%)
  starting transfers between devices  13.8 us (3%)
    unnamed x2, waiting for transfers between devices  223 us
    ppermute x4, waiting for transfers between devices, ring_gather(): earlier.append(lax.ppermute(earlier[-1], axis, up))  84.2 us
    gather x4, local copies, waits for them, and re-layouts, add_block(): int_flat[int_pick]  31.3 us
    unnamed x36, local copies, waits for them, and re-layouts  21.5 us
    scatter-add x4, other arithmetic, add_block(): return (partial_value.at[target_pick].add(products), None)  17.5 us
    dot_general x4, matrix products, add_block(): jnp.einsum('bxy,byz->bxz', amp_flat[amp_pick], int_flat[int_pick], precis...  17.2 us
    ppermute x4, starting transfers between devices, ring_gather(): earlier.append(lax.ppermute(earlier[-1], axis, up))  10.5 us
  transfers between devices with their start and end apart: 8, of which 7 were waited for; matrix products, arithmetic and copies ran while one was open for 2% of the time, Pallas kernels for 0%

profile of v1, /device:TPU:1, one launch (start us, length us, event | category | flops | bytes accessed | tf_op | source)
XLA Modules:
  0.0 453.2 jit_solution(12098027820226899846)
XLA Ops:
  6.5 3.0 collective-permute-start
  9.6 23.3 %collective-permute-done = f32[2,4,256,256]{3,2,1,0:T(8,128)S(1)} collective-permute-done((f32[2,4,256,256]{3,2,1,0:T(8,128)}, f32[2,4,256,256]{3,2,1,0:T(8,128)S(1)}, u32[]{:S(2)}, u32[]{:S(2)}) %collective-permute-start) | collective-permute-done | bytes 2097184 | tf_op jit(solution)/shard_map/ppermute | solution.py:13
  34.2 2.4 collective-permute-start.1
  36.9 22.7 %collective-permute-done.1 = f32[2,4,256,256]{3,2,1,0:T(8,128)S(1)} collective-permute-done((f32[2,4,256,256]{3,2,1,0:T(8,128)S(1)}, f32[2,4,256,256]{3,2,1,0:T(8,128)S(1)}, u32[]{:S(2)}, u32[]{:S(2)}) %collective-permute-start.1) | collective-permute-done | bytes 2097184 | tf_op jit(solution)/shard_map/ppermute | solution.py:13
  59.6 2.5 collective-permute-start.2
  65.1 19.9 %collective-permute-done.2 = f32[2,4,256,256]{3,2,1,0:T(8,128)} collective-permute-done((f32[2,4,256,256]{3,2,1,0:T(8,128)S(1)}, f32[2,4,256,256]{3,2,1,0:T(8,128)}, u32[]{:S(2)}, u32[]{:S(2)}) %collective-permute-start.2) | collective-permute-done | bytes 2097184 | tf_op jit(solution)/shard_map/ppermute | solution.py:13
  85.0 2.6 collective-permute-start.3
  87.6 2.1 collective-permute-done.5
  92.6 18.3 %collective-permute-done.3 = f32[2,4,256,256]{3,2,1,0:T(8,128)} collective-permute-done((f32[2,4,256,256]{3,2,1,0:T(8,128)}, f32[2,4,256,256]{3,2,1,0:T(8,128)}, u32[]{:S(2)}, u32[]{:S(2)}) %collective-permute-start.3) | collective-permute-done | bytes 2097184 | tf_op jit(solution)/shard_map/ppermute | solution.py:13
  114.5 2.0 constant_dynamic-update-slice_fusion.13
  116.5 2.0 constant_dynamic-update-slice_fusion.12
  130.5 6.3 %constant_dynamic-slice_fusion.3 = f32[2,32,256,256]{3,2,1,0:T(8,128)} fusion(f32[2,64,256,256]{3,2,1,0:T(8,128)S(1)} %constant_dynamic-update-slice_fusion, s32[]{:T(128)S(6)} %select_n.81), kind=kLoop, calls=%fused_computation.71 | loop fusion | bytes 33554436 | tf_op jit(solution)/shard_map/jit(_roll_dynamic)/dynamic_slice | solution.py:17
  136.8 7.8 %broadcast_in_dim.2 = f32[64,256,256]{2,1,0:T(8,128)} broadcast(f32[]{:T(128)} %constant.89.clone.1), dimensions={} | broadcast | bytes 16777220 | tf_op jit(solution)/shard_map/broadcast_in_dim | solution.py:60
  144.6 74.3 %while.10 = (s32[]{:T(128)}, f32[64,256,256]{2,1,0:T(8,128)}, s32[4,8]{1,0:T(4,128)S(1)}, s32[4,8]{1,0:T(4,128)S(1)}, f32[4,256,256]{2,1,0:T(8,128)S(1)}, /*inde...) while((s32[]{:T(128)}, f32[64,256,256]{2,1,0:T(8,128)}, s32[4,8]{1,0:T(4,128)S(1)}, ...), condition=%wide.region_2.3_spmd, body=%wide.region_0.2_spmd.sunk | while | flops 1611139200 | bytes 20980156 | solution.py:62
  144.6 2.0 gather_fusion
  146.7 7.8 %gather_fusion.1 = f32[8,256,256]{2,1,0:T(8,128)} fusion(f32[64,256,256]{2,1,0:T(8,128)} %get-tuple-element.133, s32[1024]{0:T(1024)S(1)} %pad_clamp_fusion.5), kind=kCustom, calls=%fused_computation.1.clone.1 | custom fusion | bytes 4194336 | tf_op jit(solution)/shard_map/while/body/eval_jaxpr/gather | solution.py:54
  154.5 4.3 fusion.34
  158.8 4.4 scatter_fusion
  163.2 2.0 gather_fusion
  165.2 7.8 %gather_fusion.1 = f32[8,256,256]{2,1,0:T(8,128)} fusion(f32[64,256,256]{2,1,0:T(8,128)} %get-tuple-element.133, s32[1024]{0:T(1024)S(1)} %pad_clamp_fusion.5), kind=kCustom, calls=%fused_computation.1.clone.1 | custom fusion | bytes 4194336 | tf_op jit(solution)/shard_map/while/body/eval_jaxpr/gather | solution.py:54
  173.1 4.3 fusion.34
  177.4 4.4 scatter_fusion
  181.8 2.0 gather_fusion
  183.8 7.8 %gather_fusion.1 = f32[8,256,256]{2,1,0:T(8,128)} fusion(f32[64,256,256]{2,1,0:T(8,128)} %get-tuple-element.133, s32[1024]{0:T(1024)S(1)} %pad_clamp_fusion.5), kind=kCustom, calls=%fused_computation.1.clone.1 | custom fusion | bytes 4194336 | tf_op jit(solution)/shard_map/while/body/eval_jaxpr/gather | solution.py:54
  191.7 4.3 fusion.34
  196.0 4.4 scatter_fusion
  200.4 2.0 gather_fusion
  202.4 7.8 %gather_fusion.1 = f32[8,256,256]{2,1,0:T(8,128)} fusion(f32[64,256,256]{2,1,0:T(8,128)} %get-tuple-element.133, s32[1024]{0:T(1024)S(1)} %pad_clamp_fusion.5), kind=kCustom, calls=%fused_computation.1.clone.1 | custom fusion | bytes 4194336 | tf_op jit(solution)/shard_map/while/body/eval_jaxpr/gather | solution.py:54
  210.2 4.3 fusion.34
  214.6 4.4 scatter_fusion
  220.8 223.1 %all-reduce.3.cloned.1.call-done = f32[2,32,256,256]{3,2,1,0:T(8,128)} async-done(((f32[2,32,256,256]{3,2,1,0:T(8,128)}), f32[2,32,256,256]{3,2,1,0:T(8,128)}) %all-reduce.3.cloned.1.call-update) | async-done | bytes 16777232
  444.0 2.3 dynamic-slice_add_fusion
  (64 shorter events, 24.3 us)
Async XLA Ops:
  6.5 112.0 %copy-start.1 = (f32[2,4,256,256]{3,2,1,0:T(8,128)S(1)}, f32[2,4,256,256]{3,2,1,0:T(8,128)}, u32[]{:S(2)}) copy-start(f32[2,4,256,256]{3,2,1,0:T(8,128)} %param.7) | copy-start | bytes 6291460
  6.5 437.4 %all-reduce.3.cloned.1.call-start = ((), (), s32[]{:S(2)}) async-start(), calls=%async_computation | async-start | bytes 33554432
  6.5 26.3 %collective-permute-start = (f32[2,4,256,256]{3,2,1,0:T(8,128)}, f32[2,4,256,256]{3,2,1,0:T(8,128)S(1)}, u32[]{:S(2)}, u32[]{:S(2)}) collective-permute-start(f32[2,4,256,256]{3,2,1,0:T(8,128)} %param.7), channel_id=1, source_target_pairs={{0,16},{16,32},{32,48},{48,64},{64,80},{80,96},{96,112},{112,0},{1... | collective-permute-start | bytes 6291464 | tf_op jit(solution)/shard_map/ppermute | solution.py:13
  32.9 1.3 copy-start.2
  34.2 25.4 %collective-permute-start.1 = (f32[2,4,256,256]{3,2,1,0:T(8,128)S(1)}, f32[2,4,256,256]{3,2,1,0:T(8,128)S(1)}, u32[]{:S(2)}, u32[]{:S(2)}) collective-permute-start(f32[2,4,256,256]{3,2,1,0:T(8,128)S(1)} %collective-permute-done), channel_id=1, source_target_pairs={{0,16},{16,32},{32,48},{48,64},{64,80},{80,96},{96,112},{112,0},{1... | collective-permute-start | bytes 6291464 | tf_op jit(solution)/shard_map/ppermute | solution.py:13
  36.6 26.0 %collective-permute-start.4 = (f32[2,4,256,256]{3,2,1,0:T(8,128)}, f32[2,4,256,256]{3,2,1,0:T(8,128)S(1)}, u32[]{:S(2)}, u32[]{:S(2)}) collective-permute-start(f32[2,4,256,256]{3,2,1,0:T(8,128)} %param.7), channel_id=1, source_target_pairs={{0,112},{16,0},{32,16},{48,32},{64,48},{80,64},{96,80},{112,96},{1... | collective-permute-start | bytes 6291464 | tf_op jit(solution)/shard_map/ppermute | solution.py:15
  59.6 30.2 %copy-start.6 = (f32[2,4,256,256]{3,2,1,0:T(8,128)}, f32[2,4,256,256]{3,2,1,0:T(8,128)S(1)}, u32[]{:S(2)}) copy-start(f32[2,4,256,256]{3,2,1,0:T(8,128)S(1)} %collective-permute-done.1) | copy-start | bytes 6291460
  59.6 25.5 %collective-permute-start.2 = (f32[2,4,256,256]{3,2,1,0:T(8,128)S(1)}, f32[2,4,256,256]{3,2,1,0:T(8,128)}, u32[]{:S(2)}, u32[]{:S(2)}) collective-permute-start(f32[2,4,256,256]{3,2,1,0:T(8,128)S(1)} %collective-permute-done.1), channel_id=1, source_target_pairs={{0,16},{16,32},{32,48},{48,64},{64,80},{80,96},{96,112},{112,0},{1... | collective-permute-start | bytes 6291464 | tf_op jit(solution)/shard_map/ppermute | solution.py:13
  62.5 1.3 copy-start.4
  63.9 25.9 %collective-permute-start.5 = (f32[2,4,256,256]{3,2,1,0:T(8,128)S(1)}, f32[2,4,256,256]{3,2,1,0:T(8,128)}, u32[]{:S(2)}, u32[]{:S(2)}) collective-permute-start(f32[2,4,256,256]{3,2,1,0:T(8,128)S(1)} %collective-permute-done.4), channel_id=1, source_target_pairs={{0,112},{16,0},{32,16},{48,32},{64,48},{80,64},{96,80},{112,96},{1... | collective-permute-start | bytes 6291464 | tf_op jit(solution)/shard_map/ppermute | solution.py:15
  85.0 25.9 %collective-permute-start.3 = (f32[2,4,256,256]{3,2,1,0:T(8,128)}, f32[2,4,256,256]{3,2,1,0:T(8,128)}, u32[]{:S(2)}, u32[]{:S(2)}) collective-permute-start(f32[2,4,256,256]{3,2,1,0:T(8,128)} %collective-permute-done.2), channel_id=1, source_target_pairs={{0,16},{16,32},{32,48},{48,64},{64,80},{80,96},{96,112},{112,0},{1... | collective-permute-start | bytes 6291464 | tf_op jit(solution)/shard_map/ppermute | solution.py:13
  89.7 30.9 %collective-permute-start.6 = (f32[2,4,256,256]{3,2,1,0:T(8,128)}, f32[2,4,256,256]{3,2,1,0:T(8,128)}, u32[]{:S(2)}, u32[]{:S(2)}) collective-permute-start(f32[2,4,256,256]{3,2,1,0:T(8,128)} %collective-permute-done.5), channel_id=1, source_target_pairs={{0,112},{16,0},{32,16},{48,32},{64,48},{80,64},{96,80},{112,96},{1... | collective-permute-start | bytes 6291464 | tf_op jit(solution)/shard_map/ppermute | solution.py:15
  92.5 26.1 %copy-start.5 = (f32[2,4,256,256]{3,2,1,0:T(8,128)S(1)}, f32[2,4,256,256]{3,2,1,0:T(8,128)}, u32[]{:S(2)}) copy-start(f32[2,4,256,256]{3,2,1,0:T(8,128)} %copy-done.4) | copy-start | bytes 6291460
  114.5 11.6 %copy-start.7 = (f32[2,4,256,256]{3,2,1,0:T(8,128)S(1)}, f32[2,4,256,256]{3,2,1,0:T(8,128)}, u32[]{:S(2)}) copy-start(f32[2,4,256,256]{3,2,1,0:T(8,128)} %copy-done.6) | copy-start | bytes 6291460
  116.5 9.8 %copy-start.3 = (f32[2,4,256,256]{3,2,1,0:T(8,128)S(1)}, f32[2,4,256,256]{3,2,1,0:T(8,128)}, u32[]{:S(2)}) copy-start(f32[2,4,256,256]{3,2,1,0:T(8,128)} %copy-done.2) | copy-start | bytes 6291460
  136.8 7.8 %copy-start = (f32[2,2,256,256]{3,2,1,0:T(8,128)S(1)}, f32[2,2,256,256]{3,2,1,0:T(8,128)}, u32[]{:S(2)}) copy-start(f32[2,2,256,256]{3,2,1,0:T(8,128)} %param.6) | copy-start | bytes 3145732
  219.0 0.7 copy-start.9
  219.0 225.0 %copy-start.8 = (f32[2,2,256,256]{3,2,1,0:T(8,128)S(1)}, f32[2,2,256,256]{3,2,1,0:T(8,128)}, u32[]{:S(2)}) copy-start(f32[2,2,256,256]{3,2,1,0:T(8,128)} %param.8) | copy-start | bytes 3145732
Sparse Core Ops, SparseCore 0:
  219.1 224.8 all-reduce.2
